TPU v7x, 128 devices: a whole 4x4x4 slice. The times are simulated.
128 devices in a mesh: section: 4 (over x_lo, core), seq: 8 (over x_hi, z), dp: 4 (over y).
Axes of the slice: x: 4 (x_hi: 2, x_lo: 2; x = x_hi * 2 + x_lo), y: 4, z: 4, core: 2. Of those that a mesh axis runs over, the one named last changes fastest.
Arguments:
- layer_input: bfloat16 [4, 8192, 16384], P('section', ('seq', 'dp')), may hold values from -6 to 6
- conv_weight: float32 [4, 4, 16384], P('section'), may hold values from -3 to 3
- conv_bias: float32 [4, 16384], P('section'), may hold values from -3 to 3
- log_decay: float32 [4, 8192, 256], P('section', ('seq', 'dp')), may hold values from -2 to 0, as said below
- state_write: bfloat16 [4, 16, 8192], P('section', None, ('seq', 'dp')), may hold values from -4 to 4
- state_read: bfloat16 [4, 16, 8192], P('section', None, ('seq', 'dp')), may hold values from -1.5 to 1.5
- skip_gain: float32 [4, 256], P('section'), may hold values from 0.5 to 2
- grad_out: bfloat16 [4, 8192, 16384], P('section', ('seq', 'dp')), may hold values from -6 to 6
Outputs:
- grad_prev: bfloat16 [4, 8192, 16384], P('section', ('seq', 'dp'))
- conv_weight_grad: float32 [4, 4, 16384], P('section', None, ('seq', 'dp'))
- conv_bias_grad: float32 [4, 16384], P('section', ('seq', 'dp'))
- skip_grad: float32 [4, 256], P('section', ('seq', 'dp'))
Inputs may be any that keep to these rules, and one draw needn't show every extreme that they name: `log_decay`: negative.
All inputs are finite; a program needn't handle non-finite values.
Results may differ from a plain program's by a relative error of at most 0.0047.
Values may be sent and summed in bfloat16 or wider, within the bound.
A program may use at most 320 MiB of HBM per device.

v0:
```python
import jax
import jax.numpy as jnp
from jax import lax
from jax.sharding import PartitionSpec as P

STRETCH = 256


HIGH = lax.Precision.HIGHEST
group_heads = 32


def from_behind(block, axis, distance):
    devices = range(lax.axis_size(axis))
    route = [(i - distance, i) for i in devices if i - distance in devices]
    return lax.ppermute(block, axis, route)


def carried_in(part, axis, combine, identity):
    count = lax.axis_size(axis)
    place = lax.axis_index(axis)
    ahead = count - 1 - place
    gathered = jax.tree.map(lambda a: lax.all_gather(a, axis), part)
    state = jax.tree.map(lambda a, e: jnp.zeros_like(a) + jnp.asarray(e, a.dtype), part, identity)

    def one(hop, state):
        source = count - 1 - hop
        return combine(
            state, jax.tree.map(lambda a: lax.dynamic_index_in_dim(a, source, 0, False), gathered)
        )

    return lax.fori_loop(0, ahead, one, state)


def silu_slope(pre_act):
    sigma = jax.nn.sigmoid(pre_act)
    return sigma * (1.0 + pre_act * (1.0 - sigma))


def later_first(earlier, later):
    decay_high, state_high = earlier
    decay_low, state_low = later
    return (decay_low * decay_high, state_low + decay_low[:, None, None] * state_high)


def block_product(writes, readers, cumulative, upstream):
    scores = lax.dot_general(
        writes, readers, (((0,), (0,)), ((), ())), preferred_element_type=jnp.float32
    )
    span_len = scores.shape[0]
    row_ids = lax.broadcasted_iota(jnp.int32, (span_len, span_len), 0)
    col_ids = lax.broadcasted_iota(jnp.int32, (span_len, span_len), 1)
    causal = col_ids >= row_ids
    head_count = cumulative.shape[1]
    group_size = min(group_heads, head_count)
    pieces = []
    for first_head in range(0, head_count, group_size):
        head_rates = cumulative[:, first_head : first_head + group_size].T
        spread = head_rates[:, None, :] - head_rates[:, :, None]
        weights = jnp.where(
            causal[None], jnp.exp(jnp.minimum(spread, 0.0)) * scores[None], 0.0
        ).astype(jnp.bfloat16)
        pieces.append(
            jnp.einsum(
                "hst,thp->shp",
                weights,
                upstream[:, first_head : first_head + group_size, :],
                preferred_element_type=jnp.float32,
            )
        )
    return jnp.concatenate(pieces, axis=1)


def block_summary(readers, cumulative, upstream):
    weighted = (readers.astype(jnp.float32)[None, :, :] * jnp.exp(cumulative).T[:, None, :]).astype(
        jnp.bfloat16
    )
    return jnp.einsum("hnt,thp->hnp", weighted, upstream, preferred_element_type=jnp.float32)


def on_device(
    layer_input, conv_weight, conv_bias, log_decay, state_write, state_read, skip_gain, grad_out
):
    inputs = layer_input[0]
    weight = conv_weight[0]
    bias_row = conv_bias[0]
    decay_rates = log_decay[0]
    writes = state_write[0]
    readers = state_read[0]
    skip_row = skip_gain[0]
    upstream = grad_out[0]
    token_count, channels = inputs.shape
    head_count = decay_rates.shape[1]
    head_size = channels // head_count
    state_size = writes.shape[0]
    tap_count = weight.shape[0]
    prior_rows = from_behind(inputs[token_count - (tap_count - 1) :], ("seq", "dp"), 1)
    padded = jnp.concatenate([prior_rows, inputs], axis=0)
    pre_act = jnp.broadcast_to(bias_row[None, :], (token_count, channels))
    for tap_pos in range(tap_count):
        begin = tap_count - 1 - tap_pos
        pre_act = pre_act + weight[tap_pos][None, :] * padded[begin : begin + token_count].astype(
            jnp.float32
        )
    active = jax.nn.silu(pre_act)
    blocks = token_count // STRETCH
    grad_heads = upstream.reshape(token_count, head_count, head_size)
    block_idx = 0
    cumulative = jnp.cumsum(decay_rates, axis=0)
    local_parts = [block_product(writes, readers, cumulative, grad_heads)]
    summaries = [block_summary(readers, cumulative, grad_heads)]
    cumulatives = [cumulative]
    device_decay = jnp.ones((head_count,), jnp.float32)
    device_state = jnp.zeros((head_count, state_size, head_size), jnp.float32)
    for block_idx in reversed(range(blocks)):
        device_decay, device_state = later_first(
            (device_decay, device_state),
            (jnp.exp(cumulatives[block_idx][-1]), summaries[block_idx]),
        )
    identity = (
        jnp.ones((head_count,), jnp.float32),
        jnp.zeros((head_count, state_size, head_size), jnp.float32),
    )
    carried = carried_in((device_decay, device_state), ("seq", "dp"), later_first, identity)
    carry_state = carried[1]
    outputs = [None] * blocks
    for block_idx in reversed(range(blocks)):
        cumulative = cumulatives[block_idx]
        block_total = cumulative[-1]
        carried_part = jnp.einsum(
            "ns,hnp->shp", writes.astype(jnp.float32), carry_state, precision=HIGH
        )
        carried_part = carried_part * jnp.exp(block_total[None, :] - cumulative)[:, :, None]
        outputs[block_idx] = local_parts[block_idx] + carried_part
        carry_state = jnp.exp(block_total)[:, None, None] * carry_state + summaries[block_idx]
    ssd_out = outputs[0]
    grad_act = ssd_out + skip_row[None, :, None] * grad_heads.astype(jnp.float32)
    grad_act = grad_act.reshape(token_count, channels)
    skip_term = jnp.sum(
        grad_heads.astype(jnp.float32) * active.reshape(token_count, head_count, head_size),
        axis=(0, 2),
    )
    grad_pre = grad_act * silu_slope(pre_act)
    after_rows = from_behind(grad_pre[: tap_count - 1], ("seq", "dp"), -1)
    extended = jnp.concatenate([grad_pre, after_rows], axis=0)
    input_grad = jnp.zeros((token_count, channels), jnp.float32)
    weight_terms = []
    for tap_pos in range(tap_count):
        input_grad = (
            input_grad + weight[tap_pos][None, :] * extended[tap_pos : tap_pos + token_count]
        )
        begin = tap_count - 1 - tap_pos
        weight_terms.append(
            jnp.sum(grad_pre * padded[begin : begin + token_count].astype(jnp.float32), axis=0)
        )
    weight_grad = jnp.stack(weight_terms, axis=0)
    bias_grad = jnp.sum(grad_pre, axis=0)
    shares = (
        lax.psum_scatter(weight_grad, ("seq", "dp"), scatter_dimension=1, tiled=True),
        lax.psum_scatter(bias_grad, ("seq", "dp"), scatter_dimension=0, tiled=True),
        lax.psum_scatter(skip_term, ("seq", "dp"), scatter_dimension=0, tiled=True),
    )
    passed = from_behind(input_grad.astype(jnp.bfloat16)[None], "section", -1)
    return (passed, shares[0][None], shares[1][None], shares[2][None])


def solution(mesh):
    placed = (
        P("section", ("seq", "dp"), None),
        P("section", None, None),
        P("section", None),
        P("section", ("seq", "dp"), None),
        P("section", None, ("seq", "dp")),
        P("section", None, ("seq", "dp")),
        P("section", None),
        P("section", ("seq", "dp"), None),
    )
    return jax.shard_map(
        on_device,
        mesh=mesh,
        in_specs=placed,
        out_specs=(
            P("section", ("seq", "dp"), None),
            P("section", None, ("seq", "dp")),
            P("section", ("seq", "dp")),
            P("section", ("seq", "dp")),
        ),
        check_vma=False,
    )
```

profile of v0, /device:TPU:10, one launch (start us, length us, event | category | flops | bytes accessed | tf_op | source)
XLA Modules:
  0.0 1091.7 jit_solution(16527236741669498864)
XLA Ops:
  8.5 11.9 %copy.45 = bf16[1,256,16384]{1,2,0:T(8,128)(2,1)} copy(bf16[1,256,16384]{2,1,0:T(8,128)(2,1)} %param.17) | data formatting | bytes 16777216 | tf_op args[7]
  20.7 5.7 fusion.74
  29.5 3.5 collective-permute-start
  33.8 89.7 %all-gather.1 = f32[32,1,256]{2,1,0:T(1,128)S(1)} all-gather(f32[1,1,256]{2,1,0:T(1,128)S(1)} %get-tuple-element.116), channel_id=1, replica_groups=mesh['section'=4,'seq'=8,'dp'=4] {'seq','dp'}, dimensions={0}, use_global_device_ids=true | all-gather | bytes 33792 | tf_op jit(solution)/shard_map/all_gather | solution.py:23
  124.0 3.2 bitcast_dynamic-update-slice_fusion.7
  127.2 3.3 bitcast_dynamic-update-slice_fusion.6
  130.6 3.3 bitcast_dynamic-update-slice_fusion.5
  143.4 6.8 copy-done.1
  150.4 177.7 %all-gather.4.cloned.1.call-done = f32[8192,16,64]{0,2,1:T(8,128)} async-done(((f32[256,16,64]{0,2,1:T(8,128)}), f32[8192,16,64]{0,2,1:T(8,128)}) %all-gather.4.cloned.1.call-update) | async-done | bytes 33554448 | tf_op jit(solution)/shard_map/all_gather | solution.py:23
  328.1 53.0 %copy.65 = f32[8192,16,64]{2,1,0:T(8,128)} copy(f32[8192,16,64]{0,2,1:T(8,128)} %all-gather.4.cloned.1.call-done) | data formatting | bytes 67108864 | tf_op jit(solution)/shard_map/while | solution.py:32
  381.3 64.9 %while.14 = (s32[]{:T(128)}, f32[256,16,64]{2,1,0:T(8,128)S(1)}, s32[]{:T(128)}, f32[32,256,16,64]{3,2,1,0:T(8,128)}, f32[32,256]{1,0:T(8,128)S(1)}, /*index=5*/s32[]{:T(128)}, s32[]{:T(128)}, s32[]{:T(128)}, s32[]{:T(128)}) while((s32[]{:T(128)}, f32[256,16,64]{2,1,0:T(8,128)S(1)}, s32[]{:T(128)}, f32[32,256,16,64]{3,2,1,0:T(8,128)}, ...), condition=%wide.region_3.4_spmd, body=%wide.region_2.3_spmd.sunk | while | flops 524294 | bytes 3148947 | solution.py:32
  381.3 2.1 bitcast_add_fusion.2
  383.5 2.1 bitcast_add_fusion.2
  385.7 2.1 bitcast_add_fusion.2
  387.8 2.1 bitcast_add_fusion.2
  390.0 2.1 bitcast_add_fusion.2
  392.2 2.1 bitcast_add_fusion.2
  394.3 2.1 bitcast_add_fusion.2
  396.5 2.1 bitcast_add_fusion.2
  398.7 2.1 bitcast_add_fusion.2
  400.8 2.1 bitcast_add_fusion.2
  405.1 2.1 bitcast_add_fusion.2
  407.3 2.1 bitcast_add_fusion.2
  409.5 2.1 bitcast_add_fusion.2
  411.6 2.1 bitcast_add_fusion.2
  413.8 2.1 bitcast_add_fusion.2
  418.1 2.1 bitcast_add_fusion.2
  420.3 2.1 bitcast_add_fusion.2
  422.5 2.1 bitcast_add_fusion.2
  424.6 2.1 bitcast_add_fusion.2
  426.8 2.1 bitcast_add_fusion.2
  431.1 2.1 bitcast_add_fusion.2
  433.3 2.1 bitcast_add_fusion.2
  435.5 2.1 bitcast_add_fusion.2
  437.6 2.1 bitcast_add_fusion.2
  439.8 2.1 bitcast_add_fusion.2
  441.9 2.1 bitcast_add_fusion.2
  446.3 16.8 %fusion.19 = f32[256,256,64]{0,2,1:T(8,128)} fusion(f32[256,256,64]{0,2,1:T(8,128)} %copy-done.1, bf16[256,256,64]{0,2,1:T(8,128)(2,1)} %bitcast.113, f32[256,16,64]{2,1,0:T(8,128)S(1)} %get-tuple-element.88, f32[256]{0:T(256)S(1)} %bitcast.150, f32[256,256]{0,1:T(8,128)S(1)} %copy.63, bf16[1,16,256]{2,1,0:T(8,128)(2,1)S(1)} %copy-done), kind=kOutput, calls=%fused_computation.34 | convolution fusion | flops 826277888 | bytes 43262976 | tf_op jit(solution)/shard_map/ns,hnp->shp/dot_general | solution.py:130
  463.1 17.4 %copy.64 = f32[256,16384]{1,0:T(8,128)} copy(f32[256,16384]{0,1:T(8,128)} %bitcast.121) | data formatting | bytes 33554432 | tf_op jit(solution)/shard_map/reshape | solution.py:138
  480.5 32.5 %fusion.5 = (f32[16384]{0:T(1024)S(1)}, f32[16384]{0:T(1024)S(1)}, f32[16384]{0:T(1024)S(1)}, f32[16384]{0:T(1024)}, f32[16384]{0:T(1024)S(1)}, /*index=5*/f32[256,16384]{1,0:T(8,128)}) fusion(bf16[256,16384]{1,0:T(8,128)(2,1)} %bitcast.107, bf16[3,16384]{1,0:T(4,128)(2,1)S(1)} %collective-permute-done, bf16[1,256,16384]{2,1,0:T(8,128)(2,1)} %param.10, ...), kind=kLoop, calls=%fused_computation.17 | loop fusion | flops 197050368 | bytes 51085312 | tf_op jit(solution)/shard_map/reduce_sum | solution.py:154
  514.1 4.9 collective-permute-start.1
  519.0 4.2 collective-permute-done.1
  523.2 39.3 %fusion.17 = (f32[16384]{0:T(1024)S(1)}, bf16[1,256,16384]{2,1,0:T(8,128)(2,1)}) fusion(bf16[1,256,16384]{2,1,0:T(8,128)(2,1)} %param.17, bf16[256,16384]{1,0:T(8,128)(2,1)} %bitcast.108, bf16[3,16384]{1,0:T(4,128)(2,1)S(1)} %collective-permute-done, f32[16384]{0:T(1024)S(1)} %bitcast.132, f32[16384]{0:T(1024)S(1)} %bitcast.134, f32[16384]{0:T(1024)S(1)} %bitcast.130, ...), kind=kLoop, calls=%fused_computation.31 | loop fusion | flops 163561472 | bytes 42631168 | tf_op jit(solution)/shard_map/reduce_sum | solution.py:139
  564.7 5.1 copy.66
  571.8 303.5 %all-reduce.4.cloned.1.call-done = f32[16384]{0:T(1024)} async-done(((f32[16384]{0:T(1024)}), f32[16384]{0:T(1024)}) %all-reduce.4.cloned.1.call-update) | async-done | bytes 65552
  876.8 91.8 %all-reduce.1 = f32[256]{0:T(256)S(1)} all-reduce(f32[256]{0:T(256)S(1)} %reduce_sum.68), channel_id=5, replica_groups=mesh['section'=4,'seq'=8,'dp'=4] {'seq','dp'}, use_global_device_ids=true, to_apply=%region_13.14.clone | all-reduce | flops 256 | bytes 2048
  969.3 106.6 %reduce-scatter.4.cloned.1.call-done = f32[512,4]{1,0:T(8,128)} async-done(((f32[16384,4]{1,0:T(8,128)}), f32[512,4]{1,0:T(8,128)}) %reduce-scatter.4.cloned.1.call-update) | async-done | bytes 8208
  1077.6 7.7 copy.88
  (104 shorter events, 32.1 us)
Async XLA Ops:
  7.2 116.6 %copy-start = (bf16[1,16,256]{2,1,0:T(8,128)(2,1)S(1)}, bf16[1,16,256]{2,1,0:T(8,128)(2,1)}, u32[]{:S(2)}) copy-start(bf16[1,16,256]{2,1,0:T(8,128)(2,1)} %param.14) | copy-start | bytes 24580
  7.2 320.9 %all-gather.4.cloned.1.call-start = ((), (), s32[]{:S(2)}) async-start(), calls=%async_computation.1 | async-start | bytes 34603008 | tf_op jit(solution)/shard_map/all_gather | solution.py:23
  8.5 12.1 %copy-start.4 = (bf16[1,16,256]{2,1,0:T(8,128)(2,1)S(1)}, bf16[1,16,256]{2,1,0:T(8,128)(2,1)}, u32[]{:S(2)}) copy-start(bf16[1,16,256]{2,1,0:T(8,128)(2,1)} %param.15) | copy-start | bytes 24580
  28.4 846.9 %all-reduce.4.cloned.1.call-start = ((), (), s32[]{:S(2)}) async-start(), calls=%async_computation.3 | async-start | bytes 131072
  29.5 451.0 %collective-permute-start = (bf16[3,16384]{1,0:T(4,128)(2,1)S(1)}, bf16[3,16384]{1,0:T(4,128)(2,1)S(1)}, u32[]{:S(2)}, u32[]{:S(2)}) collective-permute-start(bf16[3,16384]{1,0:T(4,128)(2,1)S(1)} %slice_bitcast_fusion.8), channel_id=1, source_target_pairs={{0,1},{1,2},{2,3},{3,4},{4,5},{5,6},{6,7},{7,8},{8,9},{9,10},{10,1... | collective-permute-start | bytes 294920 | tf_op jit(solution)/shard_map/ppermute | solution.py:16
  127.2 6.7 slice-start
  130.5 3.4 slice-start.1
  141.5 8.7 copy-start.3
  143.4 6.8 copy-start.1
  381.3 65.0 %copy-start.5 = (f32[1,256]{1,0:T(1,128)S(1)}, f32[1,256]{1,0:T(1,128)}, u32[]{:S(2)}) copy-start(f32[1,256]{1,0:T(1,128)} %param.16) | copy-start | bytes 3076
  463.1 17.4 %copy-start.2 = (f32[1,16384]{1,0:T(1,128)S(1)}, f32[1,16384]{1,0:T(1,128)}, u32[]{:S(2)}) copy-start(f32[1,16384]{1,0:T(1,128)} %param.12) | copy-start | bytes 196612
  514.1 9.1 collective-permute-start.1
  562.5 515.1 %collective-permute-start.2 = (bf16[1,256,16384]{2,1,0:T(8,128)(2,1)}, bf16[1,256,16384]{2,1,0:T(8,128)(2,1)}, u32[]{:S(2)}, u32[]{:S(2)}) collective-permute-start(bf16[1,256,16384]{2,1,0:T(8,128)(2,1)} %get-tuple-element.111), channel_id=1, source_target_pairs={{32,0},{64,32},{96,64},{33,1},{65,33},{97,65},{34,2},{66,34},{98,6... | collective-permute-start | bytes 25165832 | tf_op jit(solution)/shard_map/ppermute | solution.py:16
  564.4 511.5 %reduce-scatter.4.cloned.1.call-start = ((), (), s32[]{:S(2)}) async-start(), calls=%async_computation.2 | async-start | bytes 8650752
  564.7 5.2 copy-start.6
Sparse Core Ops, SparseCore 0:
  28.5 299.5 all-gather.3
  564.5 310.7 all-reduce.3
  877.7 198.1 reduce-scatter.3
where the time goes:
time: 1100 us; the launch traced here: 1090 us
  waiting for transfers between devices  592 us (54%)
  blocking collectives  182 us (17%)
  other arithmetic  137 us (12%)
  local copies, waits for them, and re-layouts  112 us (10%)
  matrix products  42 us (4%)
  between operations  15.4 us (1%)
    unnamed x5, waiting for transfers between devices  410 us
    all_gather x1, waiting for transfers between devices, carried_in(): gathered = jax.tree.map(lambda a: lax.all_gather(a, axis), part)  178 us
    unnamed x1, blocking collectives  91.8 us
    all_gather x1, blocking collectives, carried_in(): gathered = jax.tree.map(lambda a: lax.all_gather(a, axis), part)  89.7 us
    add x30, other arithmetic, later_first(): state_low + decay_low[:, None, None] * state_high  63.4 us
    while x1, local copies, waits for them, and re-layouts, carried_in(): return lax.fori_loop(0, ahead, one, state)  53 us
    reduce_sum x2, other arithmetic, on_device(): jnp.sum(grad_heads.astype(jnp.float32) * active.reshape(token_count, head...  39.4 us
    unnamed x27, local copies, waits for them, and re-layouts  35.2 us
  transfers between devices with their start and end apart: 6, of which 4 were waited for; matrix products, arithmetic and copies ran while one was open for 17% of the time, Pallas kernels for 0%

commit v1 on v0

--- a/solution.py
+++ b/solution.py
@@ -16,20 +16,35 @@
     return lax.ppermute(block, axis, route)
 
 
-def carried_in(part, axis, combine, identity):
+def shifted_from(part, axis, distance):
+    count = lax.axis_size(axis)
+    route = [(i + distance, i) for i in range(count) if i + distance < count]
+    return jax.tree.map(lambda a: lax.ppermute(a, axis, route), part)
+
+
+def carried_in(part, axis, combine):
+    count = lax.axis_size(axis)
+    state = shifted_from(part, axis, 1)
+    distance = 1
+    while distance < count - 1:
+        state = combine(shifted_from(state, axis, distance), state)
+        distance *= 2
+    return state
+
+
+def halving_scatter(rows, axis):
     count = lax.axis_size(axis)
     place = lax.axis_index(axis)
-    ahead = count - 1 - place
-    gathered = jax.tree.map(lambda a: lax.all_gather(a, axis), part)
-    state = jax.tree.map(lambda a, e: jnp.zeros_like(a) + jnp.asarray(e, a.dtype), part, identity)
-
-    def one(hop, state):
-        source = count - 1 - hop
-        return combine(
-            state, jax.tree.map(lambda a: lax.dynamic_index_in_dim(a, source, 0, False), gathered)
-        )
-
-    return lax.fori_loop(0, ahead, one, state)
+    mask = count // 2
+    while mask >= 1:
+        pairs = rows.reshape((2, rows.shape[0] // 2) + rows.shape[1:])
+        upper = (place // mask) % 2 == 1
+        keep = jnp.where(upper, pairs[1], pairs[0])
+        send = jnp.where(upper, pairs[0], pairs[1])
+        route = [(i, i ^ mask) for i in range(count)]
+        rows = keep + lax.ppermute(send, axis, route)
+        mask //= 2
+    return rows[0]
 
 
 def silu_slope(pre_act):
@@ -117,11 +132,7 @@
             (device_decay, device_state),
             (jnp.exp(cumulatives[block_idx][-1]), summaries[block_idx]),
         )
-    identity = (
-        jnp.ones((head_count,), jnp.float32),
-        jnp.zeros((head_count, state_size, head_size), jnp.float32),
-    )
-    carried = carried_in((device_decay, device_state), ("seq", "dp"), later_first, identity)
+    carried = carried_in((device_decay, device_state), ("seq", "dp"), later_first)
     carry_state = carried[1]
     outputs = [None] * blocks
     for block_idx in reversed(range(blocks)):
@@ -155,10 +166,22 @@
         )
     weight_grad = jnp.stack(weight_terms, axis=0)
     bias_grad = jnp.sum(grad_pre, axis=0)
+    group = ("seq", "dp")
+    parts = lax.axis_size(group)
+    width = channels // parts
+    packed = jnp.concatenate(
+        [
+            weight_grad.reshape(tap_count, parts, width).transpose(1, 0, 2).reshape(parts, tap_count * width),
+            bias_grad.reshape(parts, width),
+            skip_term.reshape(parts, head_count // parts),
+        ],
+        axis=1,
+    )
+    owned = halving_scatter(packed, group)
     shares = (
-        lax.psum_scatter(weight_grad, ("seq", "dp"), scatter_dimension=1, tiled=True),
-        lax.psum_scatter(bias_grad, ("seq", "dp"), scatter_dimension=0, tiled=True),
-        lax.psum_scatter(skip_term, ("seq", "dp"), scatter_dimension=0, tiled=True),
+        owned[: tap_count * width].reshape(tap_count, width),
+        owned[tap_count * width : (tap_count + 1) * width],
+        owned[(tap_count + 1) * width :],
     )
     passed = from_behind(input_grad.astype(jnp.bfloat16)[None], "section", -1)
     return (passed, shares[0][None], shares[1][None], shares[2][None])

time: 1100 us -> 462 us (0.42)
  waiting for transfers between devices: 592 us -> 203 us
  blocking collectives: 182 us -> 0 us
  local copies, waits for them, and re-layouts: 112 us -> 53.7 us
  other arithmetic: 137 us -> 88.7 us
  starting transfers between devices: 10.4 us -> 54.3 us
  matrix products: 42 us -> 57.3 us
  between operations: 15.4 us -> 1.33 us
    unnamed x5 -> x0, waiting for transfers between devices: 410 us -> none
    ppermute x0 -> x16, waiting for transfers between devices: none -> 197 us  [the longest x5 102 us: halving_scatter(): rows = keep + lax.ppermute(send, axis, route)]
    all_gather x1 -> x0, waiting for transfers between devices: 178 us -> none  [carried_in(): gathered = jax.tree.map(lambda a: lax.all_gather(a, axis), part)]
    unnamed x1 -> x0, blocking collectives: 91.8 us -> none
    all_gather x1 -> x0, blocking collectives: 89.7 us -> none  [carried_in(): gathered = jax.tree.map(lambda a: lax.all_gather(a, axis), part)]
    add x30 -> x5, other arithmetic: 63.4 us -> 2.78 us  [later_first(): state_low + decay_low[:, None, None] * state_high]
    while x1 -> x0, local copies, waits for them, and re-layouts: 53 us -> none  [carried_in(): return lax.fori_loop(0, ahead, one, state)]
    ppermute x0 -> x16, starting transfers between devices: none -> 46.7 us  [the longest x5 26.6 us: halving_scatter(): rows = keep + lax.ppermute(send, axis, route)]
  transfers between devices with their start and end apart: 6 -> 19, of which waited for: 4 -> 14; matrix products, arithmetic and copies ran while one was open for 17% -> 19% of each run, Pallas kernels for 0% -> 0%
where the time goes in v1:
time: 462 us; the launch traced here: 459 us
  waiting for transfers between devices  203 us (44%)
  other arithmetic  88.7 us (19%)
  matrix products  57.3 us (12%)
  starting transfers between devices  54.3 us (12%)
  local copies, waits for them, and re-layouts  53.7 us (12%)
    ppermute x5, waiting for transfers between devices, halving_scatter(): rows = keep + lax.ppermute(send, axis, route)  102 us
    ppermute x11, waiting for transfers between devices, shifted_from(): return jax.tree.map(lambda a: lax.ppermute(a, axis, route), part)  95.4 us
    reduce_sum x2, other arithmetic, on_device(): jnp.sum(grad_heads.astype(jnp.float32) * active.reshape(token_count, head...  43.5 us
    reduce_sum x1, other arithmetic, on_device(): jnp.sum(grad_pre * padded[begin:begin + token_count].astype(jnp.float32),...  39.5 us
    dot_general x8, matrix products, block_product(): jnp.einsum('hst,thp->shp', weights, upstream[:, first_head:first_head + g...  33.9 us
    ppermute x5, starting transfers between devices, halving_scatter(): rows = keep + lax.ppermute(send, axis, route)  26.6 us
    unnamed x62, local copies, waits for them, and re-layouts  20.4 us
    ppermute x11, starting transfers between devices, shifted_from(): return jax.tree.map(lambda a: lax.ppermute(a, axis, route), part)  20.2 us
  transfers between devices with their start and end apart: 19, of which 14 were waited for; matrix products, arithmetic and copies ran while one was open for 19% of the time, Pallas kernels for 0%

profile of v1, /device:TPU:10, one launch (start us, length us, event | category | flops | bytes accessed | tf_op | source)
XLA Modules:
  0.0 458.7 jit_solution(13083330038086976509)
XLA Ops:
  1.9 11.9 %copy.45 = bf16[1,256,16384]{1,2,0:T(8,128)(2,1)} copy(bf16[1,256,16384]{2,1,0:T(8,128)(2,1)} %param.15) | data formatting | bytes 16777216 | tf_op args[7]
  14.7 5.7 %fusion.74 = f32[256,16,64]{2,1,0:T(8,128)S(1)} fusion(bf16[256,256,64]{0,2,1:T(8,128)(2,1)} %bitcast.92, f32[256,256]{1,0:T(8,128)S(1)} %copy.60, f32[16,256]{1,0:T(8,128)S(1)} %bitcast_convert_fusion, f32[256]{0:T(256)S(1)} %get-tuple-element.25), kind=kOutput, calls=%fused_computation.109 | convolution fusion | flops 136577024 | bytes 9716736 | tf_op jit(solution)/shard_map/hnt,thp->hnp/dot_general | solution.py:93
  21.4 2.4 collective-permute-start
  23.7 1.7 slice_bitcast_fusion.8
  25.4 3.5 collective-permute-start.11
  28.9 3.0 collective-permute-start.1
  31.9 16.3 %collective-permute-done = f32[256,16,64]{0,2,1:T(8,128)S(1)} collective-permute-done((f32[256,16,64]{0,2,1:T(8,128)S(1)}, f32[256,16,64]{0,2,1:T(8,128)S(1)}, u32[]{:S(2)}, u32[]{:S(2)}) %collective-permute-start) | collective-permute-done | bytes 1048608 | tf_op jit(solution)/shard_map/ppermute | solution.py:22
  48.2 2.3 collective-permute-start.2
  50.5 2.5 fusion.98
  57.7 16.4 %collective-permute-done.2 = f32[256,16,64]{0,2,1:T(8,128)S(1)} collective-permute-done((f32[256,16,64]{0,2,1:T(8,128)S(1)}, f32[256,16,64]{0,2,1:T(8,128)S(1)}, u32[]{:S(2)}, u32[]{:S(2)}) %collective-permute-start.2) | collective-permute-done | bytes 1048608 | tf_op jit(solution)/shard_map/ppermute | solution.py:22
  75.0 1.4 collective-permute-start.4
  76.4 4.3 bitcast_dynamic-update-slice_fusion.7
  80.7 2.5 collective-permute-start.3
  83.2 4.2 bitcast_dynamic-update-slice_fusion.6
  88.8 16.2 %collective-permute-done.4 = f32[256,16,64]{0,2,1:T(8,128)S(1)} collective-permute-done((f32[256,16,64]{0,2,1:T(8,128)S(1)}, f32[256,16,64]{0,2,1:T(8,128)S(1)}, u32[]{:S(2)}, u32[]{:S(2)}) %collective-permute-start.4) | collective-permute-done | bytes 1048608 | tf_op jit(solution)/shard_map/ppermute | solution.py:22
  105.2 1.4 collective-permute-start.6
  106.6 4.3 bitcast_dynamic-update-slice_fusion.5
  110.9 1.4 collective-permute-start.5
  112.4 4.2 bitcast_dynamic-update-slice_fusion.4
  118.6 11.3 %collective-permute-done.6 = f32[256,16,64]{0,2,1:T(8,128)S(1)} collective-permute-done((f32[256,16,64]{0,2,1:T(8,128)S(1)}, f32[256,16,64]{0,2,1:T(8,128)S(1)}, u32[]{:S(2)}, u32[]{:S(2)}) %collective-permute-start.6) | collective-permute-done | bytes 1048608 | tf_op jit(solution)/shard_map/ppermute | solution.py:22
  130.2 1.4 collective-permute-start.8
  131.6 4.3 bitcast_dynamic-update-slice_fusion.3
  135.9 1.6 collective-permute-start.7
  137.5 4.2 bitcast_dynamic-update-slice_fusion.2
  142.4 20.9 %collective-permute-done.8 = f32[256,16,64]{0,2,1:T(8,128)S(1)} collective-permute-done((f32[256,16,64]{0,2,1:T(8,128)S(1)}, f32[256,16,64]{0,2,1:T(8,128)S(1)}, u32[]{:S(2)}, u32[]{:S(2)}) %collective-permute-start.8) | collective-permute-done | bytes 1048608 | tf_op jit(solution)/shard_map/ppermute | solution.py:22
  163.5 1.4 collective-permute-start.10
  164.9 4.3 bitcast_dynamic-update-slice_fusion.1
  169.3 4.1 bitcast_dynamic-update-slice_fusion
  174.9 7.6 %collective-permute-done.9 = f32[256]{0:T(256)S(1)} collective-permute-done((f32[256]{0:T(256)S(1)}, f32[256]{0:T(256)S(1)}, u32[]{:S(2)}, u32[]{:S(2)}) %collective-permute-start.9) | collective-permute-done | bytes 1056 | tf_op jit(solution)/shard_map/ppermute | solution.py:22
  182.5 6.0 %collective-permute-done.10 = f32[256,16,64]{0,2,1:T(8,128)} collective-permute-done((f32[256,16,64]{0,2,1:T(8,128)S(1)}, f32[256,16,64]{0,2,1:T(8,128)}, u32[]{:S(2)}, u32[]{:S(2)}) %collective-permute-start.10) | collective-permute-done | bytes 1048608 | tf_op jit(solution)/shard_map/ppermute | solution.py:22
  188.6 1.5 multiply_add_fusion
  191.3 16.8 %fusion.19 = f32[256,256,64]{0,2,1:T(8,128)} fusion(f32[256,256,64]{0,2,1:T(8,128)} %bitcast_dynamic-update-slice_fusion, bf16[256,256,64]{0,2,1:T(8,128)(2,1)} %bitcast.101, f32[256,16,64]{2,1,0:T(8,128)S(1)} %copy.62, f32[256]{0:T(256)S(1)} %bitcast.127, f32[256,256]{0,1:T(8,128)S(1)} %copy.63, bf16[1,16,256]{2,1,0:T(8,128)(2,1)S(1)} %copy-done), kind=kOutput, calls=%fused_computation.32 | convolution fusion | flops 826277888 | bytes 43262976 | tf_op jit(solution)/shard_map/ns,hnp->shp/dot_general | solution.py:141
  208.2 17.5 %copy.64 = f32[256,16384]{1,0:T(8,128)} copy(f32[256,16384]{0,1:T(8,128)} %bitcast.102) | data formatting | bytes 33554432 | tf_op jit(solution)/shard_map/reshape | solution.py:149
  225.7 39.5 %fusion.5 = (f32[16384]{0:T(1024)S(1)}, f32[16384]{0:T(1024)S(1)}, f32[16384]{0:T(1024)S(1)}, f32[16384]{0:T(1024)S(1)}, f32[16384]{0:T(1024)S(1)}, /*index=5*/f32[256,16384]{1,0:T(8,128)}) fusion(bf16[256,16384]{1,0:T(8,128)(2,1)} %bitcast.90, bf16[3,16384]{1,0:T(4,128)(2,1)} %collective-permute-done.11, bf16[1,256,16384]{2,1,0:T(8,128)(2,1)} %param.8, ...), kind=kLoop, calls=%fused_computation.15 | loop fusion | flops 197050368 | bytes 51085312 | tf_op jit(solution)/shard_map/reduce_sum | solution.py:165
  266.3 2.1 collective-permute-start.12
  268.4 6.1 %collective-permute-done.12 = f32[3,16384]{1,0:T(4,128)S(1)} collective-permute-done((f32[3,16384]{1,0:T(4,128)S(1)}, f32[3,16384]{1,0:T(4,128)S(1)}, u32[]{:S(2)}, u32[]{:S(2)}) %collective-permute-start.12) | collective-permute-done | bytes 196640 | tf_op jit(solution)/shard_map/ppermute | solution.py:16
  274.5 43.4 %fusion.17 = (f32[16384]{0:T(1024)S(1)}, bf16[1,256,16384]{2,1,0:T(8,128)(2,1)}) fusion(bf16[1,256,16384]{2,1,0:T(8,128)(2,1)} %param.15, bf16[256,16384]{1,0:T(8,128)(2,1)} %bitcast.91, bf16[3,16384]{1,0:T(4,128)(2,1)} %collective-permute-done.11, f32[16384]{0:T(1024)S(1)} %bitcast.114, f32[16384]{0:T(1024)S(1)} %bitcast.116, f32[16384]{0:T(1024)S(1)} %bitcast.112, ...), kind=kLoop, calls=%fused_computation.29 | loop fusion | flops 163561472 | bytes 42631168 | tf_op jit(solution)/shard_map/reduce_sum | solution.py:150
  317.9 1.9 collective-permute-start.13
  320.7 93.9 %collective-permute-done.14 = f32[16,2568]{1,0:T(8,128)S(1)} collective-permute-done((f32[16,2568]{1,0:T(8,128)S(1)}, f32[16,2568]{1,0:T(8,128)S(1)}, u32[]{:S(2)}, u32[]{:S(2)}) %collective-permute-start.14) | collective-permute-done | bytes 164384 | tf_op jit(solution)/shard_map/ppermute | solution.py:45
  414.7 5.4 %collective-permute-start.15 = (f32[8,2568]{1,0:T(8,128)S(1)}, f32[8,2568]{1,0:T(8,128)S(1)}, u32[]{:S(2)}, u32[]{:S(2)}) collective-permute-start(f32[8,2568]{1,0:T(8,128)S(1)} %slice_select_fusion.1), channel_id=1, source_target_pairs={{0,8},{1,9},{2,10},{3,11},{4,12},{5,13},{6,14},{7,15},{8,0},{9,1},... | collective-permute-start | bytes 246536 | tf_op jit(solution)/shard_map/ppermute | solution.py:45
  420.1 2.5 collective-permute-done.15
  422.6 4.3 collective-permute-start.16
  426.9 2.0 collective-permute-done.16
  428.9 12.7 %collective-permute-start.17 = (f32[2,2568]{1,0:T(2,128)S(1)}, f32[2,2568]{1,0:T(2,128)S(1)}, u32[]{:S(2)}, u32[]{:S(2)}) collective-permute-start(f32[2,2568]{1,0:T(2,128)S(1)} %broadcast_select_fusion), channel_id=1, source_target_pairs={{0,2},{1,3},{2,0},{3,1},{4,6},{5,7},{6,4},{7,5},{8,10},{9,11},{10,... | collective-permute-start | bytes 61640 | tf_op jit(solution)/shard_map/ppermute | solution.py:45
  441.6 1.8 collective-permute-done.17
  443.5 4.1 collective-permute-start.18
  447.6 1.7 collective-permute-done.18
  451.0 7.7 %copy.78 = bf16[1,256,16384]{2,1,0:T(8,128)(2,1)} copy(bf16[1,256,16384]{2,1,0:T(8,128)(2,1)} %collective-permute-done.13) | data formatting | bytes 16777216
  (123 shorter events, 19.8 us)
Async XLA Ops:
  0.6 52.4 %copy-start = (bf16[1,16,256]{2,1,0:T(8,128)(2,1)S(1)}, bf16[1,16,256]{2,1,0:T(8,128)(2,1)}, u32[]{:S(2)}) copy-start(bf16[1,16,256]{2,1,0:T(8,128)(2,1)} %param.12) | copy-start | bytes 24580
  1.9 12.1 %copy-start.22 = (bf16[1,16,256]{2,1,0:T(8,128)(2,1)S(1)}, bf16[1,16,256]{2,1,0:T(8,128)(2,1)}, u32[]{:S(2)}) copy-start(bf16[1,16,256]{2,1,0:T(8,128)(2,1)} %param.13) | copy-start | bytes 24580
  14.1 0.6 copy-start.23
  21.4 26.8 %collective-permute-start = (f32[256,16,64]{0,2,1:T(8,128)S(1)}, f32[256,16,64]{0,2,1:T(8,128)S(1)}, u32[]{:S(2)}, u32[]{:S(2)}) collective-permute-start(f32[256,16,64]{0,2,1:T(8,128)S(1)} %copy.61), channel_id=1, source_target_pairs={{1,0},{2,1},{3,2},{4,3},{5,4},{6,5},{7,6},{8,7},{9,8},{10,9},{11,1... | collective-permute-start | bytes 3145736 | tf_op jit(solution)/shard_map/ppermute | solution.py:22
  25.4 200.3 %collective-permute-start.11 = (bf16[3,16384]{1,0:T(4,128)(2,1)}, bf16[3,16384]{1,0:T(4,128)(2,1)}, u32[]{:S(2)}, u32[]{:S(2)}) collective-permute-start(bf16[3,16384]{1,0:T(4,128)(2,1)} %slice_bitcast_fusion.8), channel_id=1, source_target_pairs={{0,1},{1,2},{2,3},{3,4},{4,5},{5,6},{6,7},{7,8},{8,9},{9,10},{10,1... | collective-permute-start | bytes 294920 | tf_op jit(solution)/shard_map/ppermute | solution.py:16
  28.9 28.2 %collective-permute-start.1 = (f32[256]{0:T(256)}, f32[256]{0:T(256)S(1)}, u32[]{:S(2)}, u32[]{:S(2)}) collective-permute-start(f32[256]{0:T(256)} %get-tuple-element.24), channel_id=1, source_target_pairs={{1,0},{2,1},{3,2},{4,3},{5,4},{6,5},{7,6},{8,7},{9,8},{10,9},{11,1... | collective-permute-start | bytes 3080 | tf_op jit(solution)/shard_map/ppermute | solution.py:22
  48.2 25.9 %collective-permute-start.2 = (f32[256,16,64]{0,2,1:T(8,128)S(1)}, f32[256,16,64]{0,2,1:T(8,128)S(1)}, u32[]{:S(2)}, u32[]{:S(2)}) collective-permute-start(f32[256,16,64]{0,2,1:T(8,128)S(1)} %collective-permute-done), channel_id=1, source_target_pairs={{1,0},{2,1},{3,2},{4,3},{5,4},{6,5},{7,6},{8,7},{9,8},{10,9},{11,1... | collective-permute-start | bytes 3145736 | tf_op jit(solution)/shard_map/ppermute | solution.py:22
  57.1 0.6 copy-start.25
  74.9 5.8 %copy-start.26 = (f32[256]{0:T(256)S(1)}, f32[256]{0:T(256)}, u32[]{:S(2)}) copy-start(f32[256]{0:T(256)} %copy-done.25) | copy-start | bytes 3076
  75.0 8.3 %copy-start.11 = (f32[256,256]{1,0:T(8,128)S(1)}, f32[256,256]{1,0:T(8,128)}, u32[]{:S(2)}) copy-start(f32[256,256]{1,0:T(8,128)} %fusion.87) | copy-start | bytes 786436
  75.0 8.3 %copy-start.15 = (pred[256,256]{1,0:T(8,128)(4,1)S(1)}, pred[256,256]{1,0:T(8,128)(4,1)}, u32[]{:S(2)}) copy-start(pred[256,256]{1,0:T(8,128)(4,1)} %iota_compare_fusion) | copy-start | bytes 196612
  75.0 8.3 %copy-start.21 = (f32[32,256]{1,0:T(8,128)S(1)}, f32[32,256]{1,0:T(8,128)}, u32[]{:S(2)}) copy-start(f32[32,256]{1,0:T(8,128)} %copy.46) | copy-start | bytes 98308
  75.0 30.0 %collective-permute-start.4 = (f32[256,16,64]{0,2,1:T(8,128)S(1)}, f32[256,16,64]{0,2,1:T(8,128)S(1)}, u32[]{:S(2)}, u32[]{:S(2)}) collective-permute-start(f32[256,16,64]{0,2,1:T(8,128)S(1)} %multiply_add_fusion.4), channel_id=1, source_target_pairs={{2,0},{3,1},{4,2},{5,3},{6,4},{7,5},{8,6},{9,7},{10,8},{11,9},{12,... | collective-permute-start | bytes 3145736 | tf_op jit(solution)/shard_map/ppermute | solution.py:22
  80.7 6.7 %copy-start.9 = (f32[32,256]{0,1:T(8,128)S(1)}, f32[32,256]{0,1:T(8,128)}, u32[]{:S(2)}) copy-start(f32[32,256]{0,1:T(8,128)} %get-tuple-element.21) | copy-start | bytes 98308
  80.7 7.4 %copy-start.8 = (f32[32,256]{0,1:T(8,128)S(1)}, f32[32,256]{0,1:T(8,128)}, u32[]{:S(2)}) copy-start(f32[32,256]{0,1:T(8,128)} %get-tuple-element.20) | copy-start | bytes 98308
  80.7 8.1 %collective-permute-start.3 = (f32[256]{0:T(256)S(1)}, f32[256]{0:T(256)S(1)}, u32[]{:S(2)}, u32[]{:S(2)}) collective-permute-start(f32[256]{0:T(256)S(1)} %copy-done.26), channel_id=1, source_target_pairs={{1,0},{2,1},{3,2},{4,3},{5,4},{6,5},{7,6},{8,7},{9,8},{10,9},{11,1... | collective-permute-start | bytes 3080 | tf_op jit(solution)/shard_map/ppermute | solution.py:22
  105.2 7.2 %copy-start.12 = (f32[256,256]{1,0:T(8,128)S(1)}, f32[256,256]{1,0:T(8,128)}, u32[]{:S(2)}) copy-start(f32[256,256]{1,0:T(8,128)} %fusion.87) | copy-start | bytes 786436
  105.2 7.2 %copy-start.16 = (pred[256,256]{1,0:T(8,128)(4,1)S(1)}, pred[256,256]{1,0:T(8,128)(4,1)}, u32[]{:S(2)}) copy-start(pred[256,256]{1,0:T(8,128)(4,1)} %iota_compare_fusion) | copy-start | bytes 196612
  105.2 7.2 %copy-start.19 = (f32[32,256]{1,0:T(8,128)S(1)}, f32[32,256]{1,0:T(8,128)}, u32[]{:S(2)}) copy-start(f32[32,256]{1,0:T(8,128)} %copy.50) | copy-start | bytes 98308
  105.2 24.8 %collective-permute-start.6 = (f32[256,16,64]{0,2,1:T(8,128)S(1)}, f32[256,16,64]{0,2,1:T(8,128)S(1)}, u32[]{:S(2)}, u32[]{:S(2)}) collective-permute-start(f32[256,16,64]{0,2,1:T(8,128)S(1)} %multiply_add_fusion.3), channel_id=1, source_target_pairs={{4,0},{5,1},{6,2},{7,3},{8,4},{9,5},{10,6},{11,7},{12,8},{13,9},{1... | collective-permute-start | bytes 3145736 | tf_op jit(solution)/shard_map/ppermute | solution.py:22
  110.9 5.7 %copy-start.7 = (f32[32,256]{0,1:T(8,128)S(1)}, f32[32,256]{0,1:T(8,128)}, u32[]{:S(2)}) copy-start(f32[32,256]{0,1:T(8,128)} %get-tuple-element.19) | copy-start | bytes 98308
  110.9 6.4 %copy-start.6 = (f32[32,256]{0,1:T(8,128)S(1)}, f32[32,256]{0,1:T(8,128)}, u32[]{:S(2)}) copy-start(f32[32,256]{0,1:T(8,128)} %get-tuple-element.18) | copy-start | bytes 98308
  110.9 7.7 %collective-permute-start.5 = (f32[256]{0:T(256)S(1)}, f32[256]{0:T(256)S(1)}, u32[]{:S(2)}, u32[]{:S(2)}) collective-permute-start(f32[256]{0:T(256)S(1)} %mul.260), channel_id=1, source_target_pairs={{2,0},{3,1},{4,2},{5,3},{6,4},{7,5},{8,6},{9,7},{10,8},{11,9},{12,... | collective-permute-start | bytes 3080 | tf_op jit(solution)/shard_map/ppermute | solution.py:22
  130.1 7.4 %copy-start.13 = (f32[256,256]{1,0:T(8,128)S(1)}, f32[256,256]{1,0:T(8,128)}, u32[]{:S(2)}) copy-start(f32[256,256]{1,0:T(8,128)} %fusion.87) | copy-start | bytes 786436
  130.1 7.4 %copy-start.17 = (pred[256,256]{1,0:T(8,128)(4,1)S(1)}, pred[256,256]{1,0:T(8,128)(4,1)}, u32[]{:S(2)}) copy-start(pred[256,256]{1,0:T(8,128)(4,1)} %iota_compare_fusion) | copy-start | bytes 196612
  130.2 7.4 %copy-start.20 = (f32[32,256]{1,0:T(8,128)S(1)}, f32[32,256]{1,0:T(8,128)}, u32[]{:S(2)}) copy-start(f32[32,256]{1,0:T(8,128)} %copy.54) | copy-start | bytes 98308
  130.2 33.1 %collective-permute-start.8 = (f32[256,16,64]{0,2,1:T(8,128)S(1)}, f32[256,16,64]{0,2,1:T(8,128)S(1)}, u32[]{:S(2)}, u32[]{:S(2)}) collective-permute-start(f32[256,16,64]{0,2,1:T(8,128)S(1)} %multiply_add_fusion.2), channel_id=1, source_target_pairs={{8,0},{9,1},{10,2},{11,3},{12,4},{13,5},{14,6},{15,7},{16,8},{17,9... | collective-permute-start | bytes 3145736 | tf_op jit(solution)/shard_map/ppermute | solution.py:22
  135.9 5.8 %copy-start.5 = (f32[32,256]{0,1:T(8,128)S(1)}, f32[32,256]{0,1:T(8,128)}, u32[]{:S(2)}) copy-start(f32[32,256]{0,1:T(8,128)} %get-tuple-element.17) | copy-start | bytes 98308
  135.9 6.5 %collective-permute-start.7 = (f32[256]{0:T(256)S(1)}, f32[256]{0:T(256)S(1)}, u32[]{:S(2)}, u32[]{:S(2)}) collective-permute-start(f32[256]{0:T(256)S(1)} %mul.263), channel_id=1, source_target_pairs={{4,0},{5,1},{6,2},{7,3},{8,4},{9,5},{10,6},{11,7},{12,8},{13,9},{1... | collective-permute-start | bytes 3080 | tf_op jit(solution)/shard_map/ppermute | solution.py:22
  163.4 5.8 %copy-start.4 = (f32[32,256]{0,1:T(8,128)S(1)}, f32[32,256]{0,1:T(8,128)}, u32[]{:S(2)}) copy-start(f32[32,256]{0,1:T(8,128)} %get-tuple-element.16) | copy-start | bytes 98308
  163.4 5.8 %copy-start.14 = (f32[256,256]{1,0:T(8,128)S(1)}, f32[256,256]{1,0:T(8,128)}, u32[]{:S(2)}) copy-start(f32[256,256]{1,0:T(8,128)} %fusion.87) | copy-start | bytes 786436
  163.4 5.8 %copy-start.18 = (pred[256,256]{1,0:T(8,128)(4,1)S(1)}, pred[256,256]{1,0:T(8,128)(4,1)}, u32[]{:S(2)}) copy-start(pred[256,256]{1,0:T(8,128)(4,1)} %iota_compare_fusion) | copy-start | bytes 196612
  163.5 25.1 %collective-permute-start.10 = (f32[256,16,64]{0,2,1:T(8,128)S(1)}, f32[256,16,64]{0,2,1:T(8,128)}, u32[]{:S(2)}, u32[]{:S(2)}) collective-permute-start(f32[256,16,64]{0,2,1:T(8,128)S(1)} %multiply_add_fusion.1), channel_id=1, source_target_pairs={{16,0},{17,1},{18,2},{19,3},{20,4},{21,5},{22,6},{23,7},{24,8},{25... | collective-permute-start | bytes 3145736 | tf_op jit(solution)/shard_map/ppermute | solution.py:22
  169.2 5.5 %copy-start.24 = (f32[1,256]{1,0:T(1,128)S(1)}, f32[1,256]{1,0:T(1,128)}, u32[]{:S(2)}) copy-start(f32[1,256]{1,0:T(1,128)} %copy-done.23) | copy-start | bytes 3076
  169.3 22.1 %copy-start.27 = (f32[1,256]{1,0:T(1,128)S(1)}, f32[1,256]{1,0:T(1,128)}, u32[]{:S(2)}) copy-start(f32[1,256]{1,0:T(1,128)} %param.14) | copy-start | bytes 3076
  173.4 9.1 %collective-permute-start.9 = (f32[256]{0:T(256)S(1)}, f32[256]{0:T(256)S(1)}, u32[]{:S(2)}, u32[]{:S(2)}) collective-permute-start(f32[256]{0:T(256)S(1)} %mul.266), channel_id=1, source_target_pairs={{8,0},{9,1},{10,2},{11,3},{12,4},{13,5},{14,6},{15,7},{16,8},{17,9... | collective-permute-start | bytes 3080 | tf_op jit(solution)/shard_map/ppermute | solution.py:22
  208.2 17.5 %copy-start.2 = (f32[1,1,16384]{2,1,0:T(1,128)S(1)}, f32[1,1,16384]{2,1,0:T(1,128)}, u32[]{:S(2)}) copy-start(f32[1,1,16384]{2,1,0:T(1,128)} %get-tuple-element.14) | copy-start | bytes 196612
  208.2 17.5 %copy-start.3 = (f32[1,1,16384]{2,1,0:T(1,128)S(1)}, f32[1,1,16384]{2,1,0:T(1,128)}, u32[]{:S(2)}) copy-start(f32[1,1,16384]{2,1,0:T(1,128)} %get-tuple-element.15) | copy-start | bytes 196612
  208.2 17.5 %copy-start.10 = (f32[1,16384]{1,0:T(1,128)S(1)}, f32[1,16384]{1,0:T(1,128)}, u32[]{:S(2)}) copy-start(f32[1,16384]{1,0:T(1,128)} %param.10) | copy-start | bytes 196612
  266.3 8.3 %collective-permute-start.12 = (f32[3,16384]{1,0:T(4,128)S(1)}, f32[3,16384]{1,0:T(4,128)S(1)}, u32[]{:S(2)}, u32[]{:S(2)}) collective-permute-start(f32[3,16384]{1,0:T(4,128)S(1)} %slice.238), channel_id=1, source_target_pairs={{1,0},{2,1},{3,2},{4,3},{5,4},{6,5},{7,6},{8,7},{9,8},{10,9},{11,1... | collective-permute-start | bytes 589832 | tf_op jit(solution)/shard_map/ppermute | solution.py:16
  317.9 133.1 %collective-permute-start.13 = (bf16[1,256,16384]{2,1,0:T(8,128)(2,1)}, bf16[1,256,16384]{2,1,0:T(8,128)(2,1)}, u32[]{:S(2)}, u32[]{:S(2)}) collective-permute-start(bf16[1,256,16384]{2,1,0:T(8,128)(2,1)} %get-tuple-element.11), channel_id=1, source_target_pairs={{32,0},{64,32},{96,64},{33,1},{65,33},{97,65},{34,2},{66,34},{98,6... | collective-permute-start | bytes 25165832 | tf_op jit(solution)/shard_map/ppermute | solution.py:16
  320.6 94.1 %collective-permute-start.14 = (f32[16,2568]{1,0:T(8,128)S(1)}, f32[16,2568]{1,0:T(8,128)S(1)}, u32[]{:S(2)}, u32[]{:S(2)}) collective-permute-start(f32[16,2568]{1,0:T(8,128)S(1)} %slice_select_fusion), channel_id=1, source_target_pairs={{0,16},{1,17},{2,18},{3,19},{4,20},{5,21},{6,22},{7,23},{8,24},{9,... | collective-permute-start | bytes 493064 | tf_op jit(solution)/shard_map/ppermute | solution.py:45
  414.7 7.9 %collective-permute-start.15 = (f32[8,2568]{1,0:T(8,128)S(1)}, f32[8,2568]{1,0:T(8,128)S(1)}, u32[]{:S(2)}, u32[]{:S(2)}) collective-permute-start(f32[8,2568]{1,0:T(8,128)S(1)} %slice_select_fusion.1), channel_id=1, source_target_pairs={{0,8},{1,9},{2,10},{3,11},{4,12},{5,13},{6,14},{7,15},{8,0},{9,1},... | collective-permute-start | bytes 246536 | tf_op jit(solution)/shard_map/ppermute | solution.py:45
  422.6 6.3 %collective-permute-start.16 = (f32[4,2568]{1,0:T(4,128)S(1)}, f32[4,2568]{1,0:T(4,128)S(1)}, u32[]{:S(2)}, u32[]{:S(2)}) collective-permute-start(f32[4,2568]{1,0:T(4,128)S(1)} %slice_select_fusion.2), channel_id=1, source_target_pairs={{0,4},{1,5},{2,6},{3,7},{4,0},{5,1},{6,2},{7,3},{8,12},{9,13},{10,... | collective-permute-start | bytes 123272 | tf_op jit(solution)/shard_map/ppermute | solution.py:45
  428.9 14.5 %collective-permute-start.17 = (f32[2,2568]{1,0:T(2,128)S(1)}, f32[2,2568]{1,0:T(2,128)S(1)}, u32[]{:S(2)}, u32[]{:S(2)}) collective-permute-start(f32[2,2568]{1,0:T(2,128)S(1)} %broadcast_select_fusion), channel_id=1, source_target_pairs={{0,2},{1,3},{2,0},{3,1},{4,6},{5,7},{6,4},{7,5},{8,10},{9,11},{10,... | collective-permute-start | bytes 61640 | tf_op jit(solution)/shard_map/ppermute | solution.py:45
  443.5 5.8 %collective-permute-start.18 = (f32[1,2568]{1,0:T(1,128)S(1)}, f32[1,2568]{1,0:T(1,128)S(1)}, u32[]{:S(2)}, u32[]{:S(2)}) collective-permute-start(f32[1,2568]{1,0:T(1,128)S(1)} %broadcast_select_fusion.1), channel_id=1, source_target_pairs={{0,1},{1,0},{2,3},{3,2},{4,5},{5,4},{6,7},{7,6},{8,9},{9,8},{10,11... | collective-permute-start | bytes 30824 | tf_op jit(solution)/shard_map/ppermute | solution.py:45
  450.4 8.3 %copy-start.1 = (bf16[1,16,256]{2,1,0:T(8,128)(2,1)S(1)}, bf16[1,16,256]{2,1,0:T(8,128)(2,1)}, u32[]{:S(2)}) copy-start(bf16[1,16,256]{2,1,0:T(8,128)(2,1)} %param.12) | copy-start | bytes 24580

commit v2 on v1

--- a/solution.py
+++ b/solution.py
@@ -91,6 +91,24 @@
         jnp.bfloat16
     )
     return jnp.einsum("hnt,thp->hnp", weighted, upstream, preferred_element_type=jnp.float32)
+
+
+def conv_grads(grad_pre, padded, weight):
+    token_count = grad_pre.shape[0]
+    tap_count = weight.shape[0]
+    after_rows = from_behind(grad_pre[: tap_count - 1], ("seq", "dp"), -1)
+    extended = jnp.concatenate([grad_pre, after_rows], axis=0)
+    input_grad = jnp.zeros(grad_pre.shape, jnp.float32)
+    weight_terms = []
+    for tap_pos in range(tap_count):
+        input_grad = (
+            input_grad + weight[tap_pos][None, :] * extended[tap_pos : tap_pos + token_count]
+        )
+        begin = tap_count - 1 - tap_pos
+        weight_terms.append(
+            jnp.sum(grad_pre * padded[begin : begin + token_count].astype(jnp.float32), axis=0)
+        )
+    return input_grad, jnp.stack(weight_terms, axis=0), jnp.sum(grad_pre, axis=0)
 
 
 def on_device(
@@ -132,40 +150,27 @@
             (device_decay, device_state),
             (jnp.exp(cumulatives[block_idx][-1]), summaries[block_idx]),
         )
-    carried = carried_in((device_decay, device_state), ("seq", "dp"), later_first)
-    carry_state = carried[1]
-    outputs = [None] * blocks
-    for block_idx in reversed(range(blocks)):
-        cumulative = cumulatives[block_idx]
-        block_total = cumulative[-1]
-        carried_part = jnp.einsum(
-            "ns,hnp->shp", writes.astype(jnp.float32), carry_state, precision=HIGH
-        )
-        carried_part = carried_part * jnp.exp(block_total[None, :] - cumulative)[:, :, None]
-        outputs[block_idx] = local_parts[block_idx] + carried_part
-        carry_state = jnp.exp(block_total)[:, None, None] * carry_state + summaries[block_idx]
-    ssd_out = outputs[0]
-    grad_act = ssd_out + skip_row[None, :, None] * grad_heads.astype(jnp.float32)
-    grad_act = grad_act.reshape(token_count, channels)
     skip_term = jnp.sum(
         grad_heads.astype(jnp.float32) * active.reshape(token_count, head_count, head_size),
         axis=(0, 2),
     )
-    grad_pre = grad_act * silu_slope(pre_act)
-    after_rows = from_behind(grad_pre[: tap_count - 1], ("seq", "dp"), -1)
-    extended = jnp.concatenate([grad_pre, after_rows], axis=0)
-    input_grad = jnp.zeros((token_count, channels), jnp.float32)
-    weight_terms = []
-    for tap_pos in range(tap_count):
-        input_grad = (
-            input_grad + weight[tap_pos][None, :] * extended[tap_pos : tap_pos + token_count]
-        )
-        begin = tap_count - 1 - tap_pos
-        weight_terms.append(
-            jnp.sum(grad_pre * padded[begin : begin + token_count].astype(jnp.float32), axis=0)
-        )
-    weight_grad = jnp.stack(weight_terms, axis=0)
-    bias_grad = jnp.sum(grad_pre, axis=0)
+    slope = silu_slope(pre_act)
+    cumulative = cumulatives[0]
+    block_total = cumulative[-1]
+    local_act = local_parts[0] + skip_row[None, :, None] * grad_heads.astype(jnp.float32)
+    early = conv_grads(local_act.reshape(token_count, channels) * slope, padded, weight)
+    early = lax.optimization_barrier((early, skip_term))
+    carried = carried_in((device_decay, device_state), ("seq", "dp"), later_first)
+    carry_state = carried[1]
+    carried_part = jnp.einsum(
+        "ns,hnp->shp", writes.astype(jnp.float32), carry_state, precision=HIGH
+    )
+    carried_part = carried_part * jnp.exp(block_total[None, :] - cumulative)[:, :, None]
+    late = conv_grads(carried_part.reshape(token_count, channels) * slope, padded, weight)
+    (early_input, early_weight, early_bias), skip_term = early
+    input_grad = early_input + late[0]
+    weight_grad = early_weight + late[1]
+    bias_grad = early_bias + late[2]
     group = ("seq", "dp")
     parts = lax.axis_size(group)
     width = channels // parts

time: 462 us -> 604 us (1.31); the launches traced: 459 us -> 594 us
  other arithmetic: 88.7 us -> 200 us
  local copies, waits for them, and re-layouts: 53.7 us -> 102 us
  matrix products: 57.3 us -> 46.1 us
  waiting for transfers between devices: 203 us -> 195 us
    add x0 -> x3, other arithmetic: none -> 44.7 us  [the longest x1 44.5 us: conv_grads(): input_grad + weight[tap_pos][None, :] * extended[tap_pos:tap_pos + token_...]
    broadcast_in_dim x0 -> x1, other arithmetic: none -> 44.6 us  [on_device(): passed = from_behind(input_grad.astype(jnp.bfloat16)[None], 'section', -1)]
    reduce_sum x1, other arithmetic: 39.5 us -> 68.4 us  [conv_grads(): jnp.sum(grad_pre * padded[begin:begin + token_count].astype(jnp.float32),...]
    mul x0 -> x3, local copies, waits for them, and re-layouts: none -> 20.4 us  [the longest x1 20.2 us: on_device(): carried_part * jnp.exp(block_total[None, :] - cumulative)[:, :, None]]
    slice x2 -> x5, local copies, waits for them, and re-layouts: 3.55 us -> 23 us  [the longest x4 22.8 us: conv_grads(): after_rows = from_behind(grad_pre[:tap_count - 1], ('seq', 'dp'), -1)]
    reshape x1 -> x0, local copies, waits for them, and re-layouts: 17.5 us -> none  [on_device(): grad_act = grad_act.reshape(token_count, channels)]
    unnamed x62 -> x37, local copies, waits for them, and re-layouts: 20.4 us -> 36.6 us
    ppermute x11, waiting for transfers between devices: 95.4 us -> 81 us  [shifted_from(): return jax.tree.map(lambda a: lax.ppermute(a, axis, route), part)]
  transfers between devices with their start and end apart: 19 -> 20, of which waited for: 14 -> 13; matrix products, arithmetic and copies ran while one was open for 19% -> 26% of each run, Pallas kernels for 0% -> 0%
where the time goes in v2:
time: 604 us; the launch traced here: 594 us
  other arithmetic  200 us (33%)
  waiting for transfers between devices  195 us (32%)
  local copies, waits for them, and re-layouts  102 us (17%)
  starting transfers between devices  49.8 us (8%)
  matrix products  46.1 us (8%)
    ppermute x5, waiting for transfers between devices, halving_scatter(): rows = keep + lax.ppermute(send, axis, route)  114 us
    ppermute x11, waiting for transfers between devices, shifted_from(): return jax.tree.map(lambda a: lax.ppermute(a, axis, route), part)  81 us
    reduce_sum x1, other arithmetic, conv_grads(): jnp.sum(grad_pre * padded[begin:begin + token_count].astype(jnp.float32),...  68.4 us
    broadcast_in_dim x1, other arithmetic, on_device(): passed = from_behind(input_grad.astype(jnp.bfloat16)[None], 'section', -1)  44.6 us
    add x1, other arithmetic, conv_grads(): input_grad + weight[tap_pos][None, :] * extended[tap_pos:tap_pos + token_...  44.5 us
    unnamed x37, local copies, waits for them, and re-layouts  36.6 us
    reduce_sum x2, other arithmetic, on_device(): jnp.sum(grad_heads.astype(jnp.float32) * active.reshape(token_count, head...  35 us
    dot_general x8, matrix products, block_product(): jnp.einsum('hst,thp->shp', weights, upstream[:, first_head:first_head + g...  33.5 us
  transfers between devices with their start and end apart: 20, of which 13 were waited for; matrix products, arithmetic and copies ran while one was open for 26% of the time, Pallas kernels for 0%

profile of v2, /device:TPU:10, one launch (start us, length us, event | category | flops | bytes accessed | tf_op | source)
XLA Modules:
  0.0 594.3 jit_solution(774211093347065297)
XLA Ops:
  0.7 12.0 %copy.47 = bf16[1,256,16384]{1,2,0:T(8,128)(2,1)} copy(bf16[1,256,16384]{2,1,0:T(8,128)(2,1)} %param.15) | data formatting | bytes 16777216 | tf_op args[7]
  13.8 5.7 fusion.87
  19.5 2.0 copy.68
  21.5 2.3 collective-permute-start.2
  23.8 1.9 collective-permute-start.3
  27.4 3.9 collective-permute-start
  32.2 16.2 %collective-permute-done.2 = f32[256,16,64]{0,2,1:T(8,128)S(1)} collective-permute-done((f32[256,16,64]{0,2,1:T(8,128)}, f32[256,16,64]{0,2,1:T(8,128)S(1)}, u32[]{:S(2)}, u32[]{:S(2)}) %collective-permute-start.2) | collective-permute-done | bytes 1048608 | tf_op jit(solution)/shard_map/ppermute | solution.py:22
  48.5 2.3 collective-permute-start.4
  50.8 4.2 bitcast_dynamic-update-slice_fusion.7
  55.0 4.1 bitcast_dynamic-update-slice_fusion.6
  61.1 13.4 %collective-permute-done.4 = f32[256,16,64]{0,2,1:T(8,128)} collective-permute-done((f32[256,16,64]{0,2,1:T(8,128)S(1)}, f32[256,16,64]{0,2,1:T(8,128)}, u32[]{:S(2)}, u32[]{:S(2)}) %collective-permute-start.4) | collective-permute-done | bytes 1048608 | tf_op jit(solution)/shard_map/ppermute | solution.py:22
  77.3 4.3 bitcast_dynamic-update-slice_fusion.5
  81.6 2.3 collective-permute-start.5
  83.9 4.2 bitcast_dynamic-update-slice_fusion.4
  88.9 17.0 %collective-permute-done.6 = f32[256,16,64]{0,2,1:T(8,128)} collective-permute-done((f32[256,16,64]{0,2,1:T(8,128)S(1)}, f32[256,16,64]{0,2,1:T(8,128)}, u32[]{:S(2)}, u32[]{:S(2)}) %collective-permute-start.6) | collective-permute-done | bytes 1048608 | tf_op jit(solution)/shard_map/ppermute | solution.py:22
  108.7 4.2 bitcast_dynamic-update-slice_fusion.3
  114.4 4.2 bitcast_dynamic-update-slice_fusion.2
  118.6 2.0 collective-permute-done.7
  120.7 11.5 %collective-permute-done.8 = f32[256,16,64]{0,2,1:T(8,128)} collective-permute-done((f32[256,16,64]{0,2,1:T(8,128)S(1)}, f32[256,16,64]{0,2,1:T(8,128)}, u32[]{:S(2)}, u32[]{:S(2)}) %collective-permute-start.8) | collective-permute-done | bytes 1048608 | tf_op jit(solution)/shard_map/ppermute | solution.py:22
  133.7 1.8 collective-permute-start.10
  135.5 4.1 bitcast_dynamic-update-slice_fusion.1
  139.7 4.1 bitcast_dynamic-update-slice_fusion
  143.9 11.9 %copy.63 = bf16[1,256,16384]{1,2,0:T(8,128)(2,1)} copy(bf16[1,256,16384]{2,1,0:T(8,128)(2,1)} %param.8) | data formatting | bytes 16777216 | tf_op args[0]
  157.1 4.2 collective-permute-done.9
  163.0 16.5 %collective-permute-done.11 = f32[256]{0:T(256)S(1)} collective-permute-done((f32[256]{0:T(256)S(1)}, f32[256]{0:T(256)S(1)}, u32[]{:S(2)}, u32[]{:S(2)}) %collective-permute-start.11) | collective-permute-done | bytes 1056 | tf_op jit(solution)/shard_map/ppermute | solution.py:22
  179.5 3.5 copy.64
  185.9 34.8 %fusion.2 = (f32[16384]{0:T(1024)S(1)}, f32[256,16384]{0,1:T(8,128)}) fusion(bf16[1,256,16384]{1,2,0:T(8,128)(2,1)} %copy.47, bf16[256,16384]{0,1:T(8,128)(2,1)} %bitcast.108, bf16[3,16384]{0,1:T(8,128)(2,1)} %copy.64, f32[16384]{0:T(1024)S(1)} %bitcast.119, f32[16384]{0:T(1024)S(1)} %bitcast.122, f32[16384]{0:T(1024)S(1)} %bitcast.116, ...), kind=kLoop, calls=%fused_computation.24 | loop fusion | flops 117424128 | bytes 34045952 | tf_op jit(solution)/shard_map/reduce_sum | solution.py:153
  221.1 6.8 %bitcast_multiply_fusion.1 = f32[256,256,64]{0,1,2:T(8,128)S(1)} fusion(f32[256,256]{0,1:T(8,128)S(1)} %copy.70, f32[256,16,64]{0,2,1:T(8,128)S(1)} %multiply_add_fusion, bf16[1,16,256]{2,1,0:T(8,128)(2,1)S(1)} %copy-done), kind=kOutput, calls=%fused_computation.58 | convolution fusion | flops 809500672 | bytes 18096128 | tf_op jit(solution)/shard_map/ns,hnp->shp/dot_general | solution.py:165
  227.8 20.2 %copy.71 = f32[256,256,64]{0,2,1:T(8,128)} copy(f32[256,256,64]{0,1,2:T(8,128)S(1)} %bitcast_multiply_fusion.1) | data formatting | bytes 33554432 | tf_op jit(solution)/shard_map/mul | solution.py:168
  248.0 68.4 %fusion.9 = (f32[16384]{0:T(1024)S(1)}, f32[16384]{0:T(1024)S(1)}, f32[16384]{0:T(1024)S(1)}, f32[16384]{0:T(1024)S(1)}, f32[16384]{0:T(1024)S(1)}, /*index=5*/f...) fusion(bf16[256,16384]{0,1:T(8,128)(2,1)} %bitcast.109, ...), kind=kLoop, calls=%fused_computation.31 | loop fusion | flops 213745664 | bytes 109871104 | tf_op jit(solution)/shard_map/reduce_sum | solution.py:109
  316.4 6.1 %slice.260 = f32[3,16384]{0,1:T(8,128)} slice(f32[256,16384]{0,1:T(8,128)} %get-tuple-element.38), slice={[0:3], [0:16384]} | slice | bytes 393216 | tf_op jit(solution)/shard_map/slice | solution.py:99
  322.5 5.4 copy.65
  327.9 1.9 collective-permute-start.1
  329.9 5.9 slice.266
  335.7 5.4 copy.72
  341.2 1.9 collective-permute-start.13
  343.4 5.1 copy.66
  348.4 44.5 %fusion.27 = f32[256,16384]{0,1:T(8,128)} fusion(f32[256,16384]{0,1:T(8,128)} %get-tuple-element.38, f32[3,16384]{0,1:T(8,128)} %copy.66, f32[16384]{0:T(1024)S(1)} %bitcast.120, f32[16384]{0:T(1024)S(1)} %bitcast.123, f32[16384]{0:T(1024)S(1)} %bitcast.117, f32[16384]{0:T(1024)S(1)} %bitcast.114), kind=kLoop, calls=%fused_computation.49 | loop fusion | flops 41943040 | bytes 34013184 | tf_op jit(solution)/shard_map/add | solution.py:105
  392.9 5.1 copy.73
  397.9 44.6 %fusion.35 = bf16[1,256,16384]{1,2,0:T(8,128)(2,1)} fusion(f32[256,16384]{0,1:T(8,128)} %fusion.27, f32[3,16384]{0,1:T(8,128)} %copy.73, f32[256,16384]{0,1:T(8,128)} %get-tuple-element.37, f32[16384]{0:T(1024)S(1)} %bitcast.121, f32[16384]{0:T(1024)S(1)} %bitcast.124, f32[16384]{0:T(1024)S(1)} %bitcast.118, f32[16384]{0:T(1024)S(1)} %bitcast.115), kind=kLoop, calls=%fused_computation.76 | loop fusion | flops 50331648 | bytes 42401792 | tf_op jit(solution)/shard_map/broadcast_in_dim | solution.py:191
  442.5 1.9 collective-permute-start.14
  445.0 21.2 %collective-permute-start.15 = (f32[16,2568]{1,0:T(8,128)S(1)}, f32[16,2568]{1,0:T(8,128)S(1)}, u32[]{:S(2)}, u32[]{:S(2)}) collective-permute-start(f32[16,2568]{1,0:T(8,128)S(1)} %slice_select_fusion), channel_id=1, source_target_pairs={{0,16},{1,17},{2,18},{3,19},{4,20},{5,21},{6,22},{7,23},{8,24},{9,... | collective-permute-start | bytes 493064 | tf_op jit(solution)/shard_map/ppermute | solution.py:45
  466.2 94.6 %collective-permute-done.15 = f32[16,2568]{1,0:T(8,128)S(1)} collective-permute-done((f32[16,2568]{1,0:T(8,128)S(1)}, f32[16,2568]{1,0:T(8,128)S(1)}, u32[]{:S(2)}, u32[]{:S(2)}) %collective-permute-start.15) | collective-permute-done | bytes 164384 | tf_op jit(solution)/shard_map/ppermute | solution.py:45
  561.1 5.9 %collective-permute-done.16 = f32[8,2568]{1,0:T(8,128)S(1)} collective-permute-done((f32[8,2568]{1,0:T(8,128)S(1)}, f32[8,2568]{1,0:T(8,128)S(1)}, u32[]{:S(2)}, u32[]{:S(2)}) %collective-permute-start.16) | collective-permute-done | bytes 82208 | tf_op jit(solution)/shard_map/ppermute | solution.py:45
  567.2 4.0 collective-permute-done.17
  571.3 5.3 collective-permute-done.18
  576.7 3.7 collective-permute-done.19
  582.1 11.9 %copy.74 = bf16[1,256,16384]{2,1,0:T(8,128)(2,1)} copy(bf16[1,256,16384]{1,2,0:T(8,128)(2,1)} %collective-permute-done.14) | data formatting | bytes 16777216
  (111 shorter events, 24.0 us)
Async XLA Ops:
  0.6 31.4 %copy-start = (bf16[1,16,256]{2,1,0:T(8,128)(2,1)S(1)}, bf16[1,16,256]{2,1,0:T(8,128)(2,1)}, u32[]{:S(2)}) copy-start(bf16[1,16,256]{2,1,0:T(8,128)(2,1)} %param.12) | copy-start | bytes 24580
  0.6 12.0 %copy-start.2 = (f32[1,256,256]{2,1,0:T(8,128)S(1)}, f32[1,256,256]{2,1,0:T(8,128)}, u32[]{:S(2)}) copy-start(f32[1,256,256]{2,1,0:T(8,128)} %param.11) | copy-start | bytes 786436
  0.7 13.1 %copy-start.9 = (bf16[1,16,256]{2,1,0:T(8,128)(2,1)S(1)}, bf16[1,16,256]{2,1,0:T(8,128)(2,1)}, u32[]{:S(2)}) copy-start(bf16[1,16,256]{2,1,0:T(8,128)(2,1)} %param.13) | copy-start | bytes 24580
  12.6 18.7 %copy-start.3 = (f32[1,4,16384]{2,1,0:T(4,128)S(1)}, f32[1,4,16384]{2,1,0:T(4,128)}, u32[]{:S(2)}) copy-start(f32[1,4,16384]{2,1,0:T(4,128)} %param.9) | copy-start | bytes 786436
  13.0 18.3 %copy-start.10 = (f32[1,256]{1,0:T(1,128)}, f32[1,256]{1,0:T(1,128)S(1)}, u32[]{:S(2)}) copy-start(f32[1,256]{1,0:T(1,128)S(1)} %slice.265) | copy-start | bytes 3076
  21.5 27.0 %collective-permute-start.2 = (f32[256,16,64]{0,2,1:T(8,128)}, f32[256,16,64]{0,2,1:T(8,128)S(1)}, u32[]{:S(2)}, u32[]{:S(2)}) collective-permute-start(f32[256,16,64]{0,2,1:T(8,128)} %copy.68), channel_id=1, source_target_pairs={{1,0},{2,1},{3,2},{4,3},{5,4},{6,5},{7,6},{8,7},{9,8},{10,9},{11,1... | collective-permute-start | bytes 3145736 | tf_op jit(solution)/shard_map/ppermute | solution.py:22
  23.8 36.7 %collective-permute-start.3 = (f32[256]{0:T(256)}, f32[256]{0:T(256)S(1)}, u32[]{:S(2)}, u32[]{:S(2)}) collective-permute-start(f32[256]{0:T(256)} %get-tuple-element.51), channel_id=1, source_target_pairs={{1,0},{2,1},{3,2},{4,3},{5,4},{6,5},{7,6},{8,7},{9,8},{10,9},{11,1... | collective-permute-start | bytes 3080 | tf_op jit(solution)/shard_map/ppermute | solution.py:22
  27.4 152.1 %collective-permute-start = (bf16[3,16384]{1,0:T(4,128)(2,1)}, bf16[3,16384]{1,0:T(4,128)(2,1)S(1)}, u32[]{:S(2)}, u32[]{:S(2)}) collective-permute-start(bf16[3,16384]{1,0:T(4,128)(2,1)} %slice_bitcast_fusion.8), channel_id=1, source_target_pairs={{0,1},{1,2},{2,3},{3,4},{4,5},{5,6},{6,7},{7,8},{8,9},{9,10},{10,1... | collective-permute-start | bytes 294920 | tf_op jit(solution)/shard_map/ppermute | solution.py:16
  32.0 27.2 %copy-start.5 = (pred[256,256]{1,0:T(8,128)(4,1)}, pred[256,256]{1,0:T(8,128)(4,1)S(1)}, u32[]{:S(2)}) copy-start(pred[256,256]{1,0:T(8,128)(4,1)S(1)} %iota_compare_fusion) | copy-start | bytes 196612
  48.5 26.0 %collective-permute-start.4 = (f32[256,16,64]{0,2,1:T(8,128)S(1)}, f32[256,16,64]{0,2,1:T(8,128)}, u32[]{:S(2)}, u32[]{:S(2)}) collective-permute-start(f32[256,16,64]{0,2,1:T(8,128)S(1)} %collective-permute-done.2), channel_id=1, source_target_pairs={{1,0},{2,1},{3,2},{4,3},{5,4},{6,5},{7,6},{8,7},{9,8},{10,9},{11,1... | collective-permute-start | bytes 3145736 | tf_op jit(solution)/shard_map/ppermute | solution.py:22
  60.5 23.4 %copy-start.6 = (pred[256,256]{1,0:T(8,128)(4,1)S(1)}, pred[256,256]{1,0:T(8,128)(4,1)}, u32[]{:S(2)}) copy-start(pred[256,256]{1,0:T(8,128)(4,1)} %copy-done.5) | copy-start | bytes 196612
  60.5 23.4 %copy-start.8 = (f32[32,256]{1,0:T(8,128)S(1)}, f32[32,256]{1,0:T(8,128)}, u32[]{:S(2)}) copy-start(f32[32,256]{1,0:T(8,128)} %copy.52) | copy-start | bytes 98308
  60.5 0.6 copy-start.12
  74.5 7.1 %copy-start.13 = (f32[256]{0:T(256)S(1)}, f32[256]{0:T(256)}, u32[]{:S(2)}) copy-start(f32[256]{0:T(256)} %copy-done.12) | copy-start | bytes 3076
  76.0 30.0 %collective-permute-start.6 = (f32[256,16,64]{0,2,1:T(8,128)S(1)}, f32[256,16,64]{0,2,1:T(8,128)}, u32[]{:S(2)}, u32[]{:S(2)}) collective-permute-start(f32[256,16,64]{0,2,1:T(8,128)S(1)} %multiply_add_fusion.4), channel_id=1, source_target_pairs={{2,0},{3,1},{4,2},{5,3},{6,4},{7,5},{8,6},{9,7},{10,8},{11,9},{12,... | collective-permute-start | bytes 3145736 | tf_op jit(solution)/shard_map/ppermute | solution.py:22
  81.6 7.4 %collective-permute-start.5 = (f32[256]{0:T(256)S(1)}, f32[256]{0:T(256)S(1)}, u32[]{:S(2)}, u32[]{:S(2)}) collective-permute-start(f32[256]{0:T(256)S(1)} %copy-done.13), channel_id=1, source_target_pairs={{1,0},{2,1},{3,2},{4,3},{5,4},{6,5},{7,6},{8,7},{9,8},{10,9},{11,1... | collective-permute-start | bytes 3080 | tf_op jit(solution)/shard_map/ppermute | solution.py:22
  107.5 24.8 %collective-permute-start.8 = (f32[256,16,64]{0,2,1:T(8,128)S(1)}, f32[256,16,64]{0,2,1:T(8,128)}, u32[]{:S(2)}, u32[]{:S(2)}) collective-permute-start(f32[256,16,64]{0,2,1:T(8,128)S(1)} %multiply_add_fusion.3), channel_id=1, source_target_pairs={{4,0},{5,1},{6,2},{7,3},{8,4},{9,5},{10,6},{11,7},{12,8},{13,9},{1... | collective-permute-start | bytes 3145736 | tf_op jit(solution)/shard_map/ppermute | solution.py:22
  113.0 22.5 %copy-start.7 = (pred[256,256]{1,0:T(8,128)(4,1)S(1)}, pred[256,256]{1,0:T(8,128)(4,1)}, u32[]{:S(2)}) copy-start(pred[256,256]{1,0:T(8,128)(4,1)} %copy-done.5) | copy-start | bytes 196612
  113.0 7.7 %collective-permute-start.7 = (f32[256]{0:T(256)S(1)}, f32[256]{0:T(256)S(1)}, u32[]{:S(2)}, u32[]{:S(2)}) collective-permute-start(f32[256]{0:T(256)S(1)} %mul.332), channel_id=1, source_target_pairs={{2,0},{3,1},{4,2},{5,3},{6,4},{7,5},{8,6},{9,7},{10,8},{11,9},{12,... | collective-permute-start | bytes 3080 | tf_op jit(solution)/shard_map/ppermute | solution.py:22
  133.7 10.1 %copy-start.11 = (f32[1,256]{1,0:T(1,128)S(1)}, f32[1,256]{1,0:T(1,128)}, u32[]{:S(2)}) copy-start(f32[1,256]{1,0:T(1,128)} %copy-done.10) | copy-start | bytes 3076
  133.7 49.4 %collective-permute-start.10 = (f32[256,16,64]{0,2,1:T(8,128)S(1)}, f32[256,16,64]{0,2,1:T(8,128)}, u32[]{:S(2)}, u32[]{:S(2)}) collective-permute-start(f32[256,16,64]{0,2,1:T(8,128)S(1)} %multiply_add_fusion.2), channel_id=1, source_target_pairs={{8,0},{9,1},{10,2},{11,3},{12,4},{13,5},{14,6},{15,7},{16,8},{17,9... | collective-permute-start | bytes 3145736 | tf_op jit(solution)/shard_map/ppermute | solution.py:22
  143.8 19.0 %copy-start.14 = (f32[1,256]{1,0:T(1,128)S(1)}, f32[1,256]{1,0:T(1,128)}, u32[]{:S(2)}) copy-start(f32[1,256]{1,0:T(1,128)} %param.14) | copy-start | bytes 3076
  143.9 42.0 %copy-start.4 = (f32[1,16384]{1,0:T(1,128)S(1)}, f32[1,16384]{1,0:T(1,128)}, u32[]{:S(2)}) copy-start(f32[1,16384]{1,0:T(1,128)} %param.10) | copy-start | bytes 196612
  155.8 5.5 collective-permute-start.9
  161.4 18.2 %collective-permute-start.11 = (f32[256]{0:T(256)S(1)}, f32[256]{0:T(256)S(1)}, u32[]{:S(2)}, u32[]{:S(2)}) collective-permute-start(f32[256]{0:T(256)S(1)} %mul.338), channel_id=1, source_target_pairs={{8,0},{9,1},{10,2},{11,3},{12,4},{13,5},{14,6},{15,7},{16,8},{17,9... | collective-permute-start | bytes 3080 | tf_op jit(solution)/shard_map/ppermute | solution.py:22
  184.6 36.4 %collective-permute-start.12 = (f32[256,16,64]{0,2,1:T(8,128)S(1)}, f32[256,16,64]{0,2,1:T(8,128)S(1)}, u32[]{:S(2)}, u32[]{:S(2)}) collective-permute-start(f32[256,16,64]{0,2,1:T(8,128)S(1)} %multiply_add_fusion.1), channel_id=1, source_target_pairs={{16,0},{17,1},{18,2},{19,3},{20,4},{21,5},{22,6},{23,7},{24,8},{25... | collective-permute-start | bytes 3145736 | tf_op jit(solution)/shard_map/ppermute | solution.py:22
  327.9 15.4 %collective-permute-start.1 = (f32[3,16384]{1,0:T(4,128)S(1)}, f32[3,16384]{1,0:T(4,128)S(1)}, u32[]{:S(2)}, u32[]{:S(2)}) collective-permute-start(f32[3,16384]{1,0:T(4,128)S(1)} %copy.65), channel_id=1, source_target_pairs={{1,0},{2,1},{3,2},{4,3},{5,4},{6,5},{7,6},{8,7},{9,8},{10,9},{11,1... | collective-permute-start | bytes 589832 | tf_op jit(solution)/shard_map/ppermute | solution.py:16
  341.2 51.7 %collective-permute-start.13 = (f32[3,16384]{1,0:T(4,128)S(1)}, f32[3,16384]{1,0:T(4,128)S(1)}, u32[]{:S(2)}, u32[]{:S(2)}) collective-permute-start(f32[3,16384]{1,0:T(4,128)S(1)} %copy.72), channel_id=1, source_target_pairs={{1,0},{2,1},{3,2},{4,3},{5,4},{6,5},{7,6},{8,7},{9,8},{10,9},{11,1... | collective-permute-start | bytes 589832 | tf_op jit(solution)/shard_map/ppermute | solution.py:16
  397.9 196.1 %copy-start.1 = (bf16[1,16,256]{2,1,0:T(8,128)(2,1)S(1)}, bf16[1,16,256]{2,1,0:T(8,128)(2,1)}, u32[]{:S(2)}) copy-start(bf16[1,16,256]{2,1,0:T(8,128)(2,1)} %param.12) | copy-start | bytes 24580
  442.5 139.6 %collective-permute-start.14 = (bf16[1,256,16384]{1,2,0:T(8,128)(2,1)}, bf16[1,256,16384]{1,2,0:T(8,128)(2,1)}, u32[]{:S(2)}, u32[]{:S(2)}) collective-permute-start(bf16[1,256,16384]{1,2,0:T(8,128)(2,1)} %fusion.35), channel_id=1, source_target_pairs={{32,0},{64,32},{96,64},{33,1},{65,33},{97,65},{34,2},{66,34},{98,6... | collective-permute-start | bytes 25165832 | tf_op jit(solution)/shard_map/ppermute | solution.py:16
  445.0 115.8 %collective-permute-start.15 = (f32[16,2568]{1,0:T(8,128)S(1)}, f32[16,2568]{1,0:T(8,128)S(1)}, u32[]{:S(2)}, u32[]{:S(2)}) collective-permute-start(f32[16,2568]{1,0:T(8,128)S(1)} %slice_select_fusion), channel_id=1, source_target_pairs={{0,16},{1,17},{2,18},{3,19},{4,20},{5,21},{6,22},{7,23},{8,24},{9,... | collective-permute-start | bytes 493064 | tf_op jit(solution)/shard_map/ppermute | solution.py:45
  560.9 6.1 %collective-permute-start.16 = (f32[8,2568]{1,0:T(8,128)S(1)}, f32[8,2568]{1,0:T(8,128)S(1)}, u32[]{:S(2)}, u32[]{:S(2)}) collective-permute-start(f32[8,2568]{1,0:T(8,128)S(1)} %slice_select_fusion.1), channel_id=1, source_target_pairs={{0,8},{1,9},{2,10},{3,11},{4,12},{5,13},{6,14},{7,15},{8,0},{9,1},... | collective-permute-start | bytes 246536 | tf_op jit(solution)/shard_map/ppermute | solution.py:45
  567.0 4.1 collective-permute-start.17
  571.2 5.4 collective-permute-start.18
  576.6 3.8 collective-permute-start.19
